TPU v7x, 128 devices: a whole 4x4x4 slice. The times are simulated.
128 devices in a mesh: ctx: 32 (over x, y, core), heads: 4 (over z).
Axes of the slice: x: 4, y: 4, z: 4, core: 2. Of those that a mesh axis runs over, the one named last changes fastest.
Arguments:
- queries: bfloat16 [32, 32768, 128], P('heads', 'ctx'), may hold values from -6 to 6
- keys: bfloat16 [32, 32768, 128], P('heads', 'ctx'), may hold values from -6 to 6
- values: bfloat16 [32, 32768, 128], P('heads', 'ctx'), may hold values from -6 to 6
- out_grad: bfloat16 [32, 32768, 128], P('heads', 'ctx'), may hold values from -6 to 6
- level_table: float32 [64, 16], replicated, may hold values from 0.2 to 2
- table_index: int32 [32768], P('ctx'), may hold values from 0 to 63
Outputs:
- attention_out: bfloat16 [32, 32768, 128], P('heads', 'ctx')
- query_grad: bfloat16 [32, 32768, 128], P('heads', 'ctx')
- key_grad: bfloat16 [32, 32768, 128], P('heads', 'ctx')
- value_grad: bfloat16 [32, 32768, 128], P('heads', 'ctx')
- table_grad: float32 [64, 16], replicated
All inputs are finite; a program needn't handle non-finite values.
Results may differ from a plain program's by a relative error of at most 0.0058.
Values sent between devices are 32-bit elements; how exact they have to be, the bound alone decides.
A program may use at most 256 MiB of HBM per device.

v0:
```python
import math
import jax
import jax.numpy as jnp
from jax import lax
from jax.sharding import PartitionSpec as P


def level_grid(length):
    row_ids = lax.broadcasted_iota(jnp.int32, (length, length), 0)
    col_ids = lax.broadcasted_iota(jnp.int32, (length, length), 1)
    crossed = jnp.bitwise_xor(row_ids, col_ids)
    levels = jnp.zeros((length, length), jnp.int32)
    for bit_pos in range(length.bit_length()):
        levels = levels + (crossed >= 1 << bit_pos).astype(jnp.int32)
    return (levels, col_ids <= row_ids)


def lookup(level_table, table_index):
    matches = table_index[:, None] == jnp.arange(level_table.shape[0], dtype=jnp.int32)[None, :]
    lam_all = jnp.sum(jnp.where(matches[:, :, None], level_table[None], 0.0), 1)
    return (matches, lam_all)


def block_start(queries, keys, values, out_grad, lam_tok, block_id, level_bits, factor):
    first_cross = queries.shape[1].bit_length()
    states = jnp.einsum("htd,hte->hde", keys, values, preferred_element_type=jnp.float32)
    pieces = []
    for bit_num in range(level_bits):
        scaled = (lam_tok[:, first_cross + bit_num][None, :, None] * out_grad).astype(jnp.bfloat16)
        upper_half = jnp.right_shift(block_id, bit_num) & 1 == 1
        bucket_grad = factor * jnp.einsum(
            "htd,hte->hde", queries, scaled, preferred_element_type=jnp.float32
        )
        pieces.append(jnp.where(upper_half, bucket_grad, jnp.zeros_like(bucket_grad)))
    return (states, jnp.stack(pieces))


def block_finish(queries, keys, values, out_grad, lam_tok, bucket, state_grad, factor):
    length = queries.shape[1]
    level_bits = bucket.shape[0]
    first_cross = length.bit_length()
    levels, causal = level_grid(length)
    weight = jnp.zeros((length, length), jnp.float32)
    for level_id in range(first_cross):
        weight = weight + jnp.where(levels == level_id, lam_tok[:, level_id : level_id + 1], 0.0)
    weight = factor * jnp.where(causal, weight, 0.0)
    dot_scores = jnp.einsum("htd,hsd->hts", queries, keys, preferred_element_type=jnp.float32)
    weighted = (weight[None] * dot_scores).astype(jnp.bfloat16)
    out_local = jnp.einsum("hts,hsd->htd", weighted, values, preferred_element_type=jnp.float32)
    grad_weighted = jnp.einsum("htd,hsd->hts", out_grad, values, preferred_element_type=jnp.float32)
    grad_scores = (weight[None] * grad_weighted).astype(jnp.bfloat16)
    query_local = jnp.einsum("hts,hsd->htd", grad_scores, keys, preferred_element_type=jnp.float32)
    key_local = jnp.einsum("hts,htd->hsd", grad_scores, queries, preferred_element_type=jnp.float32)
    value_local = jnp.einsum("hts,htd->hsd", weighted, out_grad, preferred_element_type=jnp.float32)
    weight_grad = jnp.sum(dot_scores * grad_weighted, 0)
    lam_cross = lam_tok[:, first_cross : first_cross + level_bits].T[:, None, :, None]
    cross = jnp.einsum("htd,jhde->jhte", queries, bucket, preferred_element_type=jnp.float32)
    attention_out = out_local + factor * jnp.sum(lam_cross * cross, 0)
    back_cross = jnp.einsum("hte,jhde->jhtd", out_grad, bucket, preferred_element_type=jnp.float32)
    query_grad = query_local + factor * jnp.sum(lam_cross * back_cross, 0)
    key_grad = key_local + jnp.einsum(
        "hte,hde->htd", values, state_grad, preferred_element_type=jnp.float32
    )
    value_grad = value_local + jnp.einsum(
        "htd,hde->hte", keys, state_grad, preferred_element_type=jnp.float32
    )
    local_cols = [
        factor * jnp.sum(jnp.where(causal & (levels == level_id), weight_grad, 0.0), 1)
        for level_id in range(first_cross)
    ]
    lam_local = jnp.stack(local_cols, 1)
    lam_far = factor * jnp.sum(cross * out_grad.astype(jnp.float32)[None], axis=(1, 3))
    spare = jnp.zeros((length, lam_tok.shape[1] - first_cross - level_bits), jnp.float32)
    lam_grad = jnp.concatenate([lam_local, lam_far.T, spare], 1)
    return (
        attention_out.astype(jnp.bfloat16),
        query_grad.astype(jnp.bfloat16),
        key_grad.astype(jnp.bfloat16),
        value_grad.astype(jnp.bfloat16),
        lam_grad,
    )


def in_bucket(owners, block_id, bit_num):
    same_top = jnp.right_shift(owners, bit_num + 1) == jnp.right_shift(block_id, bit_num + 1)
    owner_low = jnp.right_shift(owners, bit_num) & 1 == 0
    mine_high = jnp.right_shift(block_id, bit_num) & 1 == 1
    return same_top & owner_low & mine_high


def body(queries, keys, values, out_grad, level_table, table_index):
    head_local, length, head_width = queries.shape
    devices = lax.axis_size("ctx")
    level_bits = devices.bit_length() - 1
    factor = 1.0 / math.sqrt(head_width * length * devices)
    block_id = lax.axis_index("ctx")
    matches, lam_tok = lookup(level_table, table_index)
    states, grads = block_start(
        queries, keys, values, out_grad, lam_tok, block_id, level_bits, factor
    )
    shard_piece = lax.all_gather(states[None], "ctx", axis=0, tiled=True)
    owners = jnp.arange(shard_piece.shape[0], dtype=jnp.int32)
    pieces = []
    for bit_num in range(level_bits):
        member = in_bucket(owners, block_id, bit_num)
        pieces.append(jnp.sum(jnp.where(member[:, None, None, None], shard_piece, 0.0), 0))
    bucket = jnp.stack(pieces)
    bucket = bucket.astype(jnp.bfloat16)
    row_total = head_local * lax.axis_size("ctx")
    owners = jnp.arange(row_total // head_local, dtype=jnp.int32)
    term = jnp.zeros((row_total // head_local,) + states.shape, jnp.float32)
    for bit_num in range(level_bits):
        member = in_bucket(owners, block_id, bit_num)
        term = term + jnp.where(member[:, None, None, None], grads[bit_num][None], 0.0)
    state_grad = lax.psum_scatter(
        term.reshape((row_total,) + states.shape[1:]), "ctx", scatter_dimension=0, tiled=True
    )
    state_grad = state_grad.astype(jnp.bfloat16)
    attention_out, query_grad, key_grad, value_grad, lam_grad = block_finish(
        queries, keys, values, out_grad, lam_tok, bucket, state_grad, factor
    )
    table_part = jnp.sum(jnp.where(matches[:, :, None], lam_grad[:, None, :], 0.0), 0)
    table_total = lax.psum(table_part, ("ctx", "heads"))
    table_grad = table_total / math.sqrt(length * devices)
    return (attention_out, query_grad, key_grad, value_grad, table_grad)


def solution(mesh):
    placed = (
        P("heads", "ctx", None),
        P("heads", "ctx", None),
        P("heads", "ctx", None),
        P("heads", "ctx", None),
        P(),
        P("ctx"),
    )
    return jax.shard_map(
        body,
        mesh=mesh,
        in_specs=placed,
        out_specs=(
            P("heads", "ctx", None),
            P("heads", "ctx", None),
            P("heads", "ctx", None),
            P("heads", "ctx", None),
            P(),
        ),
        check_vma=False,
    )
```

profile of v0, /device:TPU:1, one launch (start us, length us, event | category | flops | bytes accessed | tf_op | source)
XLA Modules:
  0.0 370.0 jit_solution(8418169630844257545)
XLA Ops:
  7.3 0.1 broadcast_in_dim.340
  7.3 0.1 broadcast_in_dim.341
  7.4 0.1 broadcast_in_dim.335
  7.5 0.1 broadcast_in_dim.336
  7.6 0.1 broadcast_in_dim.350
  7.7 0.1 broadcast_in_dim.351
  7.9 0.1 broadcast_in_dim.346
  8.1 0.1 broadcast_in_dim.330
  8.2 0.8 copy.72
  9.0 0.9 iota_compare_fusion.1
  9.9 0.6 copy-done.7
  10.5 0.5 select_reduce_fusion.17
  11.1 2.6 fusion.100
  13.7 1.1 fusion.64
  14.9 1.1 fusion.91
  16.0 1.1 fusion.82
  17.1 1.1 fusion.73
  18.3 8.7 %fusion.2 = f32[256,128,128]{1,2,0:T(8,128)} fusion(f32[8,128,128]{1,2,0:T(8,128)S(1)} %fusion.100, f32[8,128,128]{1,2,0:T(8,128)S(1)} %fusion.91, f32[8,128,128]{1,2,0:T(8,128)S(1)} %fusion.82, f32[8,128,128]{1,2,0:T(8,128)S(1)} %fusion.73, f32[8,128,128]{1,2,0:T(8,128)S(1)} %fusion.64, pred[256]{0:T(512)(128)(4,1)S(1)} %broadcast_in_dim.351, ...), kind=kLoop, calls=%fused_computation.9 | loop fusion | flops 37748736 | bytes 19399936 | tf_op jit(solution)/shard_map/add | solution.py:114
  27.0 0.2 all-gather.3.cloned.1.call-start
  27.2 3.8 %fusion.106 = f32[8,128,128]{2,1,0:T(8,128)} fusion(bf16[8,1024,128]{2,1,0:T(8,128)(2,1)} %param.7, bf16[8,1024,128]{2,1,0:T(8,128)(2,1)} %param.8), kind=kOutput, calls=%fused_computation.153 | convolution fusion | flops 268435456 | bytes 4718592 | tf_op jit(solution)/shard_map/htd,hte->hde/dot_general | solution.py:26
  31.1 4.1 %copy.92 = f32[8,1024,128]{1,2,0:T(8,128)} copy(bf16[8,1024,128]{2,1,0:T(8,128)(2,1)} %param.9) | data formatting | bytes 6291456 | tf_op jit(solution)/shard_map/convert_element_type | solution.py:29
  35.2 21.5 %fusion.107 = f32[8,1024,1024]{2,1,0:T(8,128)} fusion(bf16[8,1024,128]{2,1,0:T(8,128)(2,1)} %param.9, bf16[8,1024,128]{2,1,0:T(8,128)(2,1)} %param.8), kind=kOutput, calls=%fused_computation.154 | convolution fusion | flops 2147483648 | bytes 37748736 | tf_op jit(solution)/shard_map/htd,hsd->hts/dot_general | solution.py:50
  56.7 30.6 %multiply_reduce_fusion = (f32[1024,1024]{1,0:T(8,128)}, f32[8,1024,1024]{2,1,0:T(8,128)}) fusion(f32[8,1024,1024]{2,1,0:T(8,128)} %fusion.107, bf16[8,1024,128]{2,1,0:T(8,128)(2,1)S(1)} %copy-done, bf16[8,1024,128]{2,1,0:T(8,128)(2,1)} %param.7), kind=kOutput, calls=%fused_computation | convolution fusion | flops 2163212288 | bytes 75497472 | tf_op jit(solution)/shard_map/htd,hsd->hts/dot_general | solution.py:47
  87.3 18.2 %select_reduce_fusion.6 = (f32[1024]{0:T(1024)S(1)}, f32[1024]{0:T(1024)S(1)}, f32[1024]{0:T(1024)S(1)}, f32[1024]{0:T(1024)S(1)}, f32[1024]{0:T(1024)S(1)}, /*i...) fusion(f32[1024,1024]{1,0:T(8,128)} %get-tuple-element.44), kind=kLoop, calls=%fused_computation.43 | loop fusion | flops 81777664 | bytes 4239360 | tf_op jit(solution)/shard_map/reduce_sum | solution.py:68
  105.6 9.6 %select_multiply_fusion = f32[1024,1024]{1,0:T(8,128)S(1)} fusion(f32[1024]{0:T(1024)S(1)} %bitcast.129, f32[1024]{0:T(1024)S(1)} %bitcast.130, f32[1024]{0:T(1024)S(1)} %bitcast.131, f32[1024]{0:T(1024)S(1)} %bitcast.132, f32[1024]{0:T(1024)S(1)} %bitcast.133, f32[1024]{0:T(1024)S(1)} %bitcast.134, f32[1024]{0:T(1024)S(1)} %bitcast.135, ...), kind=kLoop, calls=%fused_computation.55 | loop fusion | flops 71303168 | bytes 4239360 | tf_op jit(solution)/shard_map/mul | solution.py:46
  115.2 18.0 %fusion.8 = f32[8,1024,128]{2,1,0:T(8,128)} fusion(bf16[8,1024,128]{2,1,0:T(8,128)(2,1)S(1)} %copy-done, f32[8,1024,1024]{2,1,0:T(8,128)} %fusion.107, f32[1024,1024]{1,0:T(8,128)S(1)} %select_multiply_fusion), kind=kOutput, calls=%fused_computation.29 | convolution fusion | flops 2164260864 | bytes 44040192 | tf_op jit(solution)/shard_map/hts,htd->hsd/dot_general | solution.py:53
  133.2 17.5 %fusion.6 = f32[8,1024,128]{2,1,0:T(8,128)} fusion(bf16[8,1024,128]{2,1,0:T(8,128)(2,1)} %param.9, f32[8,1024,1024]{2,1,0:T(8,128)} %get-tuple-element.45, f32[1024,1024]{1,0:T(8,128)S(1)} %select_multiply_fusion), kind=kOutput, calls=%fused_computation.27 | convolution fusion | flops 2164260864 | bytes 44040192 | tf_op jit(solution)/shard_map/hts,htd->hsd/dot_general | solution.py:54
  150.8 5.1 %fusion.16 = bf16[8,1024,128]{2,1,0:T(8,128)(2,1)} fusion(f32[8,1024,128]{2,1,0:T(8,128)} %fusion.8, bf16[8,1024,128]{2,1,0:T(8,128)(2,1)} %param.8, f32[8,128,128]{1,2,0:T(8,128)} %reduce-scatter.2.cloned.1.call-done), kind=kOutput, calls=%fused_computation.39 | convolution fusion | flops 270663680 | bytes 8912896 | tf_op jit(solution)/shard_map/hte,hde->htd/dot_general | solution.py:61
  155.9 2.0 fusion.15
  158.0 62.7 %all-gather.3.cloned.1.call-done = f32[256,128,128]{2,1,0:T(8,128)} async-done(((f32[8,128,128]{2,1,0:T(8,128)}), f32[256,128,128]{2,1,0:T(8,128)}) %all-gather.3.cloned.1.call-update) | async-done | bytes 16777232 | tf_op jit(solution)/shard_map/all_gather | solution.py:101
  220.7 12.3 %select_reduce_fusion = (bf16[8,128,128]{2,1,0:T(8,128)(2,1)S(1)}, bf16[8,128,128]{2,1,0:T(8,128)(2,1)S(1)}, bf16[8,128,128]{2,1,0:T(8,128)(2,1)S(1)}, bf16[8,12...) fusion(f32[32,8,128,128]{3,2,1,0:T(8,128)} %bitcast.128, pred[32]{0:T(512)(128)(4,1)S(1)} %get-tuple-element.46, ...), kind=kLoop, calls=%fused_computation.17 | loop fusion | flops 41287680 | bytes 18088096 | tf_op jit(solution)/shard_map/reduce_sum | solution.py:106
  233.0 0.9 copy.78
  233.9 0.8 copy.77
  234.7 0.2 copy.76
  234.9 0.2 copy.75
  235.1 0.2 copy.74
  235.4 1.0 bitcast_dynamic-update-slice_fusion.1
  236.5 1.0 copy-done.9
  237.5 6.8 %multiply_reduce_fusion.1 = f32[8,128,1024]{2,1,0:T(8,128)} fusion(f32[5,1024]{1,0:T(8,128)S(1)} %slice_bitcast_fusion, bf16[5,8,128,128]{2,3,0,1:T(8,128)(2,1)S(1)} %bitcast_dynamic-update-slice_fusion, bf16[8,1024,128]{2,1,0:T(8,128)(2,1)} %param.9), kind=kOutput, calls=%fused_computation.7 | convolution fusion | flops 1351614464 | bytes 7622656 | tf_op jit(solution)/shard_map/hte,jhde->jhtd/dot_general | solution.py:59
  244.3 5.4 %copy.81 = f32[8,128,1024]{1,2,0:T(8,128)} copy(f32[8,128,1024]{2,1,0:T(8,128)} %multiply_reduce_fusion.1) | data formatting | bytes 8388608 | tf_op jit(solution)/shard_map/reduce_sum | solution.py:60
  249.7 7.2 %fusion.1 = (f32[5,1024]{1,0:T(8,128)S(1)}, f32[8,1024,128]{1,2,0:T(8,128)}) fusion(f32[8,1024,128]{1,2,0:T(8,128)} %copy.92, f32[5,1024]{1,0:T(8,128)S(1)} %slice_bitcast_fusion, bf16[5,8,128,128]{2,3,0,1:T(8,128)(2,1)S(1)} %copy-done.10, bf16[8,1024,128]{2,1,0:T(8,128)(2,1)S(1)} %copy-done), kind=kOutput, calls=%fused_computation.6 | convolution fusion | flops 1362095104 | bytes 11837440 | tf_op jit(solution)/shard_map/htd,jhde->jhte/dot_general | solution.py:57
  256.9 5.3 %copy.79 = f32[8,1024,128]{2,1,0:T(8,128)} copy(f32[8,1024,128]{1,2,0:T(8,128)} %get-tuple-element.11) | data formatting | bytes 8388608 | tf_op jit(solution)/shard_map/reduce_sum | solution.py:58
  262.2 17.4 %fusion.17 = bf16[8,1024,128]{2,1,0:T(8,128)(2,1)} fusion(f32[8,128,1024]{1,2,0:T(8,128)} %copy.81, bf16[8,1024,128]{2,1,0:T(8,128)(2,1)} %param.7, f32[8,1024,1024]{2,1,0:T(8,128)} %fusion.107, f32[1024,1024]{1,0:T(8,128)} %copy-done.1), kind=kOutput, calls=%fused_computation.41 | convolution fusion | flops 2167406592 | bytes 46137344 | tf_op jit(solution)/shard_map/hts,hsd->htd/dot_general | solution.py:52
  279.7 17.3 %add_convert_fusion = bf16[8,1024,128]{2,1,0:T(8,128)(2,1)} fusion(f32[8,1024,128]{2,1,0:T(8,128)} %copy.79, bf16[8,1024,128]{2,1,0:T(8,128)(2,1)} %param.8, f32[8,1024,1024]{2,1,0:T(8,128)} %get-tuple-element.45, f32[1024,1024]{1,0:T(8,128)} %copy-done.1), kind=kOutput, calls=%fused_computation.54 | convolution fusion | flops 2167406592 | bytes 46137344 | tf_op jit(solution)/shard_map/hts,hsd->htd/dot_general | solution.py:49
  296.9 0.1 concatenate.3
  297.0 0.5 select_reduce_fusion.5
  297.5 64.7 %psum.7 = f32[64,16]{1,0:T(8,128)S(1)} all-reduce(f32[64,16]{1,0:T(8,128)S(1)} %select_reduce_fusion.5), channel_id=1, replica_groups=mesh['ctx'=32,'heads'=4] {'ctx','heads'}, use_global_device_ids=true, to_apply=%region_23.24 | all-reduce | flops 1024 | bytes 8192 | tf_op jit(solution)/shard_map/psum | solution.py:123
  362.3 0.7 copy.93
  (43 shorter events, 0.5 us)
Async XLA Ops:
  7.2 3.9 %copy-start = (bf16[8,1024,128]{2,1,0:T(8,128)(2,1)S(1)}, bf16[8,1024,128]{2,1,0:T(8,128)(2,1)}, u32[]{:S(2)}) copy-start(bf16[8,1024,128]{2,1,0:T(8,128)(2,1)} %param.6) | copy-start | bytes 6291460
  7.2 143.6 %reduce-scatter.2.cloned.1.call-start = ((), (), s32[]{:S(2)}) async-start(), calls=%async_computation.1 | async-start | bytes 17301504 | tf_op jit(solution)/shard_map/reduce_scatter | solution.py:115
  9.0 4.8 %copy-start.3 = (bf16[8,1024,128]{2,1,0:T(8,128)(2,1)S(1)}, bf16[8,1024,128]{2,1,0:T(8,128)(2,1)}, u32[]{:S(2)}) copy-start(bf16[8,1024,128]{2,1,0:T(8,128)(2,1)} %param.9) | copy-start | bytes 6291460
  9.8 0.6 copy-start.7
  27.0 193.7 %all-gather.3.cloned.1.call-start = ((), (), s32[]{:S(2)}) async-start(), calls=%async_computation.2 | async-start | bytes 17301504 | tf_op jit(solution)/shard_map/all_gather | solution.py:101
  115.2 18.0 %copy-start.1 = (f32[1024,1024]{1,0:T(8,128)}, f32[1024,1024]{1,0:T(8,128)S(1)}, u32[]{:S(2)}) copy-start(f32[1024,1024]{1,0:T(8,128)S(1)} %select_multiply_fusion) | copy-start | bytes 12582916
  150.8 5.2 %copy-start.2 = (bf16[8,1024,128]{2,1,0:T(8,128)(2,1)S(1)}, bf16[8,1024,128]{2,1,0:T(8,128)(2,1)}, u32[]{:S(2)}) copy-start(bf16[8,1024,128]{2,1,0:T(8,128)(2,1)} %param.7) | copy-start | bytes 6291460
  150.8 5.2 %copy-start.4 = (f32[8,1024,128]{2,1,0:T(8,128)S(1)}, f32[8,1024,128]{2,1,0:T(8,128)}, u32[]{:S(2)}) copy-start(f32[8,1024,128]{2,1,0:T(8,128)} %fusion.6) | copy-start | bytes 12582916
  150.8 5.2 %copy-start.5 = (f32[8,128,128]{1,2,0:T(8,128)S(1)}, f32[8,128,128]{1,2,0:T(8,128)}, u32[]{:S(2)}) copy-start(f32[8,128,128]{1,2,0:T(8,128)} %reduce-scatter.2.cloned.1.call-done) | copy-start | bytes 1572868
  233.9 2.5 copy-start.6
  236.5 1.1 copy-start.9
  244.3 5.4 %copy-start.10 = (bf16[5,8,128,128]{2,3,0,1:T(8,128)(2,1)S(1)}, bf16[5,8,128,128]{2,3,0,1:T(8,128)(2,1)}, u32[]{:S(2)}) copy-start(bf16[5,8,128,128]{2,3,0,1:T(8,128)(2,1)} %copy-done.9) | copy-start | bytes 3932164
  279.7 17.4 %copy-start.8 = (pred[1024,64]{0,1:T(8,128)(4,1)S(1)}, pred[1024,64]{0,1:T(8,128)(4,1)}, u32[]{:S(2)}) copy-start(pred[1024,64]{0,1:T(8,128)(4,1)} %copy-done.7) | copy-start | bytes 196612
Sparse Core Ops, SparseCore 0:
  27.1 117.0 reduce-scatter.1
  147.1 73.5 all-gather.2
where the time goes:
time: 376 us; the launch traced here: 370 us
  matrix products  154 us (41%)
  blocking collectives  64.7 us (17%)
  waiting for transfers between devices  62.8 us (17%)
  other arithmetic  50.8 us (14%)
  local copies, waits for them, and re-layouts  22.4 us (6%)
  between operations  14.6 us (4%)
    psum x1, blocking collectives, body(): table_total = lax.psum(table_part, ('ctx', 'heads'))  64.7 us
    all_gather x1, waiting for transfers between devices, body(): shard_piece = lax.all_gather(states[None], 'ctx', axis=0, tiled=True)  62.7 us
    dot_general x1, matrix products, block_finish(): jnp.einsum('htd,hsd->hts', queries, keys, preferred_element_type=jnp.floa...  30.6 us
    dot_general x1, matrix products, block_finish(): jnp.einsum('htd,hsd->hts', out_grad, values, preferred_element_type=jnp.f...  21.5 us
    reduce_sum x1, other arithmetic, block_finish(): jnp.sum(jnp.where(causal & (levels == level_id), weight_grad, 0.0), 1)  18.2 us
    dot_general x1, matrix products, block_finish(): jnp.einsum('hts,htd->hsd', grad_scores, queries, preferred_element_type=j...  18 us
    dot_general x1, matrix products, block_finish(): jnp.einsum('hts,htd->hsd', weighted, out_grad, preferred_element_type=jnp...  17.5 us
    dot_general x1, matrix products, block_finish(): jnp.einsum('hts,hsd->htd', grad_scores, keys, preferred_element_type=jnp....  17.4 us
  transfers between devices with their start and end apart: 2, of which 1 were waited for; matrix products, arithmetic and copies ran while one was open for 35% of the time, Pallas kernels for 0%

commit v1 on v0

--- a/solution.py
+++ b/solution.py
@@ -98,7 +98,9 @@
     states, grads = block_start(
         queries, keys, values, out_grad, lam_tok, block_id, level_bits, factor
     )
-    shard_piece = lax.all_gather(states[None], "ctx", axis=0, tiled=True)
+    shard_piece = jnp.concatenate(
+        lax.all_to_all(jnp.stack([states[None]] * lax.axis_size("ctx")), "ctx", 0, 0), axis=0
+    )
     owners = jnp.arange(shard_piece.shape[0], dtype=jnp.int32)
     pieces = []
     for bit_num in range(level_bits):

time: 376 us -> 478 us (1.27)
  waiting for transfers between devices: 62.8 us -> 111 us
  blocking collectives: 64.7 us -> 104 us
  starting transfers between devices: 0.25 us -> 8.8 us
  local copies, waits for them, and re-layouts: 22.4 us -> 29.1 us
    all_to_all x0 -> x1, waiting for transfers between devices: none -> 111 us  [body(): lax.all_to_all(jnp.stack([states[None]] * lax.axis_size('ctx')), 'ctx', 0...]
    all_gather x1 -> x0, waiting for transfers between devices: 62.7 us -> none  [body(): shard_piece = lax.all_gather(states[None], 'ctx', axis=0, tiled=True)]
    psum x1, blocking collectives: 64.7 us -> 104 us  [body(): table_total = lax.psum(table_part, ('ctx', 'heads'))]
    all_to_all x0 -> x1, starting transfers between devices: none -> 8.76 us  [body(): lax.all_to_all(jnp.stack([states[None]] * lax.axis_size('ctx')), 'ctx', 0...]
    another operation x0 -> x1, local copies, waits for them, and re-layouts: none -> 7.83 us  [body(): jnp.stack([states[None]] * lax.axis_size('ctx'))]
  transfers between devices with their start and end apart: 2 -> 2, of which waited for: 1 -> 1; matrix products, arithmetic and copies ran while one was open for 35% -> 45% of each run, Pallas kernels for 0% -> 0%
where the time goes in v1:
time: 478 us; the launch traced here: 471 us
  matrix products  151 us (32%)
  waiting for transfers between devices  111 us (23%)
  blocking collectives  104 us (22%)
  other arithmetic  53.1 us (11%)
  local copies, waits for them, and re-layouts  29.1 us (6%)
  between operations  14.6 us (3%)
  starting transfers between devices  8.8 us (2%)
    all_to_all x1, waiting for transfers between devices, body(): lax.all_to_all(jnp.stack([states[None]] * lax.axis_size('ctx')), 'ctx', 0...  111 us
    psum x1, blocking collectives, body(): table_total = lax.psum(table_part, ('ctx', 'heads'))  104 us
    dot_general x1, matrix products, block_finish(): jnp.einsum('htd,hsd->hts', queries, keys, preferred_element_type=jnp.floa...  30.4 us
    dot_general x1, matrix products, block_finish(): jnp.einsum('htd,hsd->hts', out_grad, values, preferred_element_type=jnp.f...  20.5 us
    reduce_sum x1, other arithmetic, block_finish(): jnp.sum(jnp.where(causal & (levels == level_id), weight_grad, 0.0), 1)  18.3 us
    dot_general x1, matrix products, block_finish(): jnp.einsum('hts,htd->hsd', grad_scores, queries, preferred_element_type=j...  17.7 us
    dot_general x1, matrix products, block_finish(): jnp.einsum('hts,hsd->htd', grad_scores, keys, preferred_element_type=jnp....  17.2 us
    dot_general x1, matrix products, block_finish(): jnp.einsum('hts,hsd->htd', weighted, values, preferred_element_type=jnp.f...  17.2 us
  transfers between devices with their start and end apart: 2, of which 1 were waited for; matrix products, arithmetic and copies ran while one was open for 45% of the time, Pallas kernels for 0%

profile of v1, /device:TPU:1, one launch (start us, length us, event | category | flops | bytes accessed | tf_op | source)
XLA Modules:
  0.0 471.2 jit_solution(2475311684816523685)
XLA Ops:
  7.2 3.1 fusion.111
  10.3 7.8 %stack.20 = f32[32,1,8,128,128]{4,3,2,1,0:T(8,128)} broadcast(f32[8,128,128]{2,1,0:T(8,128)S(1)} %fusion.111), dimensions={2,3,4} | broadcast | bytes 17301504 | tf_op jit(solution)/shard_map/stack | solution.py:102
  18.2 8.8 %all-to-all-start = ((f32[32,1,8,128,128]{4,3,2,1,0:T(8,128)}), f32[32,1,8,128,128]{4,3,2,1,0:T(8,128)}, u32[]{:S(2)}, u32[]{:S(2)}) async-start(f32[32,1,8,128,128]{4,3,2,1,0:T(8,128)} %stack.20), calls=%async_computation | async-start | bytes 33554432 | tf_op jit(solution)/shard_map/all_to_all | solution.py:102
  27.1 0.1 broadcast_in_dim.337
  27.3 0.1 broadcast_in_dim.332
  27.5 0.1 broadcast_in_dim.347
  27.6 0.1 broadcast_in_dim.342
  27.8 0.1 broadcast_in_dim.326
  27.9 0.1 copy.89
  28.1 0.5 select_reduce_fusion.12
  28.7 2.6 fusion.105
  31.4 1.1 fusion.69
  32.5 1.1 fusion.96
  33.6 1.1 fusion.87
  34.8 1.1 fusion.78
  35.9 8.9 %fusion.2 = f32[256,128,128]{1,2,0:T(8,128)} fusion(f32[8,128,128]{1,2,0:T(8,128)S(1)} %fusion.105, f32[8,128,128]{1,2,0:T(8,128)S(1)} %fusion.96, f32[8,128,128]{1,2,0:T(8,128)S(1)} %fusion.87, f32[8,128,128]{1,2,0:T(8,128)S(1)} %fusion.78, f32[8,128,128]{1,2,0:T(8,128)S(1)} %fusion.69, pred[256]{0:T(512)(128)(4,1)S(1)} %broadcast_in_dim.347, ...), kind=kLoop, calls=%fused_computation.9 | loop fusion | flops 37748736 | bytes 19399936 | tf_op jit(solution)/shard_map/add | solution.py:116
  44.8 20.5 %fusion.112 = f32[8,1024,1024]{2,1,0:T(8,128)} fusion(bf16[8,1024,128]{2,1,0:T(8,128)(2,1)} %param.9, bf16[8,1024,128]{2,1,0:T(8,128)(2,1)} %param.8), kind=kOutput, calls=%fused_computation.159 | convolution fusion | flops 2147483648 | bytes 37748736 | tf_op jit(solution)/shard_map/htd,hsd->hts/dot_general | solution.py:50
  65.4 4.2 copy.109
  69.6 30.4 %multiply_reduce_fusion = (f32[1024,1024]{1,0:T(8,128)}, f32[8,1024,1024]{2,1,0:T(8,128)}) fusion(f32[8,1024,1024]{2,1,0:T(8,128)} %fusion.112, bf16[8,1024,128]{2,1,0:T(8,128)(2,1)S(1)} %copy-done, bf16[8,1024,128]{2,1,0:T(8,128)(2,1)} %param.7), kind=kOutput, calls=%fused_computation | convolution fusion | flops 2163212288 | bytes 75497472 | tf_op jit(solution)/shard_map/htd,hsd->hts/dot_general | solution.py:47
  100.0 18.3 %select_reduce_fusion.1 = (f32[1024]{0:T(1024)S(1)}, f32[1024]{0:T(1024)S(1)}, f32[1024]{0:T(1024)S(1)}, f32[1024]{0:T(1024)S(1)}, f32[1024]{0:T(1024)S(1)}, /*i...) fusion(f32[1024,1024]{1,0:T(8,128)} %get-tuple-element.44), kind=kLoop, calls=%fused_computation.48 | loop fusion | flops 81777664 | bytes 4239360 | tf_op jit(solution)/shard_map/reduce_sum | solution.py:68
  118.4 0.6 broadcast_multiply_fusion.3
  119.0 0.6 broadcast_multiply_fusion.5
  119.6 0.6 broadcast_multiply_fusion.7
  120.2 0.6 broadcast_multiply_fusion.9
  120.8 9.6 %select_multiply_fusion = f32[1024,1024]{1,0:T(8,128)S(1)} fusion(f32[1024]{0:T(1024)S(1)} %bitcast.143, f32[1024]{0:T(1024)S(1)} %bitcast.144, f32[1024]{0:T(1024)S(1)} %bitcast.145, f32[1024]{0:T(1024)S(1)} %bitcast.146, f32[1024]{0:T(1024)S(1)} %bitcast.147, f32[1024]{0:T(1024)S(1)} %bitcast.148, f32[1024]{0:T(1024)S(1)} %bitcast.149, ...), kind=kLoop, calls=%fused_computation.60 | loop fusion | flops 71303168 | bytes 4239360 | tf_op jit(solution)/shard_map/mul | solution.py:46
  130.4 17.7 %fusion.13 = f32[8,1024,128]{2,1,0:T(8,128)} fusion(bf16[8,1024,128]{2,1,0:T(8,128)(2,1)S(1)} %copy-done, f32[8,1024,1024]{2,1,0:T(8,128)} %fusion.112, f32[1024,1024]{1,0:T(8,128)S(1)} %select_multiply_fusion), kind=kOutput, calls=%fused_computation.34 | convolution fusion | flops 2164260864 | bytes 44040192 | tf_op jit(solution)/shard_map/hts,htd->hsd/dot_general | solution.py:53
  148.1 16.7 %fusion.11 = f32[8,1024,128]{2,1,0:T(8,128)} fusion(bf16[8,1024,128]{2,1,0:T(8,128)(2,1)} %param.9, f32[8,1024,1024]{2,1,0:T(8,128)} %get-tuple-element.45, f32[1024,1024]{1,0:T(8,128)S(1)} %select_multiply_fusion), kind=kOutput, calls=%fused_computation.32 | convolution fusion | flops 2164260864 | bytes 44040192 | tf_op jit(solution)/shard_map/hts,htd->hsd/dot_general | solution.py:54
  164.8 110.7 %all-to-all-done = f32[32,1,8,128,128]{4,3,2,1,0:T(8,128)} async-done(((f32[32,1,8,128,128]{4,3,2,1,0:T(8,128)}), f32[32,1,8,128,128]{4,3,2,1,0:T(8,128)}, u32[]{:S(2)}, u32[]{:S(2)}) %all-to-all-start) | async-done | bytes 16777248 | tf_op jit(solution)/shard_map/all_to_all | solution.py:102
  275.5 12.7 %fusion.10 = (bf16[8,128,128]{2,1,0:T(8,128)(2,1)S(1)}, bf16[8,128,128]{2,1,0:T(8,128)(2,1)S(1)}, bf16[8,128,128]{2,1,0:T(8,128)(2,1)S(1)}, bf16[8,128,128]{2,1,0:T(8,128)(2,1)S(1)}, bf16[8,128,128]{2,1,0:T(8,128)(2,1)S(1)}) fusion(f32[32,1,8,128,128]{4,3,2,1,0:T(8,128)} %all-to-all-done, pred[32]{0:T(512)(128)(4,1)S(1)} %get-tuple-element.46, ...), kind=kLoop, calls=%fused_computation.26 | loop fusion | flops 41287680 | bytes 18088096 | tf_op jit(solution)/shard_map/reduce_sum | solution.py:108
  288.2 0.9 copy.95
  289.1 0.8 copy.92
  289.9 0.2 copy.93
  290.1 0.2 copy.94
  290.3 0.2 copy.91
  290.5 1.0 bitcast_dynamic-update-slice_fusion.3
  291.6 1.0 copy-done.7
  292.7 6.8 %multiply_reduce_fusion.1 = f32[8,128,1024]{2,1,0:T(8,128)} fusion(f32[5,1024]{1,0:T(8,128)S(1)} %slice_bitcast_fusion, bf16[5,8,128,128]{2,3,0,1:T(8,128)(2,1)S(1)} %bitcast_dynamic-update-slice_fusion, bf16[8,1024,128]{2,1,0:T(8,128)(2,1)} %param.9), kind=kOutput, calls=%fused_computation.7 | convolution fusion | flops 1351614464 | bytes 7622656 | tf_op jit(solution)/shard_map/hte,jhde->jhtd/dot_general | solution.py:59
  299.5 5.4 %copy.98 = f32[8,128,1024]{1,2,0:T(8,128)} copy(f32[8,128,1024]{2,1,0:T(8,128)} %multiply_reduce_fusion.1) | data formatting | bytes 8388608 | tf_op jit(solution)/shard_map/reduce_sum | solution.py:60
  304.9 7.2 %fusion.1 = (f32[5,1024]{1,0:T(8,128)S(1)}, f32[8,1024,128]{1,2,0:T(8,128)}) fusion(f32[8,1024,128]{1,2,0:T(8,128)} %copy.109, f32[5,1024]{1,0:T(8,128)S(1)} %slice_bitcast_fusion, bf16[5,8,128,128]{2,3,0,1:T(8,128)(2,1)S(1)} %copy-done.8, bf16[8,1024,128]{2,1,0:T(8,128)(2,1)S(1)} %copy-done), kind=kOutput, calls=%fused_computation.6 | convolution fusion | flops 1362095104 | bytes 11837440 | tf_op jit(solution)/shard_map/htd,jhde->jhte/dot_general | solution.py:57
  312.2 5.3 %copy.96 = f32[8,1024,128]{2,1,0:T(8,128)} copy(f32[8,1024,128]{1,2,0:T(8,128)} %get-tuple-element.11) | data formatting | bytes 8388608 | tf_op jit(solution)/shard_map/reduce_sum | solution.py:58
  317.6 0.1 concatenate.3
  317.7 0.5 select_reduce_fusion
  318.2 103.6 %psum.7 = f32[64,16]{1,0:T(8,128)S(1)} all-reduce(f32[64,16]{1,0:T(8,128)S(1)} %select_reduce_fusion), channel_id=1, replica_groups=mesh['ctx'=32,'heads'=4] {'ctx','heads'}, use_global_device_ids=true, to_apply=%region_23.24 | all-reduce | flops 1024 | bytes 8192 | tf_op jit(solution)/shard_map/psum | solution.py:125
  421.8 0.7 copy.110
  422.5 17.2 %fusion.22 = bf16[8,1024,128]{2,1,0:T(8,128)(2,1)} fusion(f32[8,128,1024]{1,2,0:T(8,128)} %copy.98, bf16[8,1024,128]{2,1,0:T(8,128)(2,1)} %param.7, f32[8,1024,1024]{2,1,0:T(8,128)} %fusion.112, f32[1024,1024]{1,0:T(8,128)} %copy-done.1), kind=kOutput, calls=%fused_computation.46 | convolution fusion | flops 2167406592 | bytes 46137344 | tf_op jit(solution)/shard_map/hts,hsd->htd/dot_general | solution.py:52
  439.7 17.2 %add_convert_fusion = bf16[8,1024,128]{2,1,0:T(8,128)(2,1)} fusion(f32[8,1024,128]{2,1,0:T(8,128)} %copy.96, bf16[8,1024,128]{2,1,0:T(8,128)(2,1)} %param.8, f32[8,1024,1024]{2,1,0:T(8,128)} %get-tuple-element.45, f32[1024,1024]{1,0:T(8,128)} %copy-done.1), kind=kOutput, calls=%fused_computation.59 | convolution fusion | flops 2167406592 | bytes 46137344 | tf_op jit(solution)/shard_map/hts,hsd->htd/dot_general | solution.py:49
  457.0 5.1 %fusion.21 = bf16[8,1024,128]{2,1,0:T(8,128)(2,1)} fusion(f32[8,1024,128]{2,1,0:T(8,128)} %fusion.13, bf16[8,1024,128]{2,1,0:T(8,128)(2,1)} %param.8, f32[8,128,128]{1,2,0:T(8,128)} %reduce-scatter.2.cloned.1.call-done), kind=kOutput, calls=%fused_computation.44 | convolution fusion | flops 270663680 | bytes 8912896 | tf_op jit(solution)/shard_map/hte,hde->htd/dot_general | solution.py:61
  462.1 2.0 fusion.20
  (57 shorter events, 0.8 us)
Async XLA Ops:
  7.2 21.5 %copy-start = (bf16[8,1024,128]{2,1,0:T(8,128)(2,1)S(1)}, bf16[8,1024,128]{2,1,0:T(8,128)(2,1)}, u32[]{:S(2)}) copy-start(bf16[8,1024,128]{2,1,0:T(8,128)(2,1)} %param.6) | copy-start | bytes 6291460
  18.1 9.8 %copy-start.16 = (f32[64,16]{0,1:T(8,128)S(1)}, f32[64,16]{0,1:T(8,128)}, u32[]{:S(2)}) copy-start(f32[64,16]{0,1:T(8,128)} %param.10) | copy-start | bytes 12292
  18.1 9.9 %copy-start.17 = (s32[1024]{0:T(1024)S(1)}, s32[1024]{0:T(1024)}, u32[]{:S(2)}) copy-start(s32[1024]{0:T(1024)} %param.11) | copy-start | bytes 12292
  18.2 257.3 %all-to-all-start = ((f32[32,1,8,128,128]{4,3,2,1,0:T(8,128)}), f32[32,1,8,128,128]{4,3,2,1,0:T(8,128)}, u32[]{:S(2)}, u32[]{:S(2)}) async-start(f32[32,1,8,128,128]{4,3,2,1,0:T(8,128)} %stack.20), calls=%async_computation | async-start | bytes 33554432 | tf_op jit(solution)/shard_map/all_to_all | solution.py:102
  26.9 430.0 %reduce-scatter.2.cloned.1.call-start = ((), (), s32[]{:S(2)}) async-start(), calls=%async_computation.2 | async-start | bytes 17301504 | tf_op jit(solution)/shard_map/reduce_scatter | solution.py:117
  28.0 3.3 copy-start.3
  130.4 17.7 %copy-start.1 = (f32[1024,1024]{1,0:T(8,128)}, f32[1024,1024]{1,0:T(8,128)S(1)}, u32[]{:S(2)}) copy-start(f32[1024,1024]{1,0:T(8,128)S(1)} %select_multiply_fusion) | copy-start | bytes 12582916
  289.1 2.5 copy-start.6
  291.6 1.1 copy-start.7
  299.5 5.4 %copy-start.8 = (bf16[5,8,128,128]{2,3,0,1:T(8,128)(2,1)S(1)}, bf16[5,8,128,128]{2,3,0,1:T(8,128)(2,1)}, u32[]{:S(2)}) copy-start(bf16[5,8,128,128]{2,3,0,1:T(8,128)(2,1)} %copy-done.7) | copy-start | bytes 3932164
  312.1 5.4 %copy-start.9 = (f32[1024]{0:T(1024)S(1)}, f32[1024]{0:T(1024)}, u32[]{:S(2)}) copy-start(f32[1024]{0:T(1024)} %get-tuple-element.53) | copy-start | bytes 12292
  312.1 5.4 %copy-start.10 = (f32[1024]{0:T(1024)S(1)}, f32[1024]{0:T(1024)}, u32[]{:S(2)}) copy-start(f32[1024]{0:T(1024)} %get-tuple-element.54) | copy-start | bytes 12292
  312.1 5.4 %copy-start.11 = (f32[1024]{0:T(1024)S(1)}, f32[1024]{0:T(1024)}, u32[]{:S(2)}) copy-start(f32[1024]{0:T(1024)} %get-tuple-element.55) | copy-start | bytes 12292
  312.1 5.4 %copy-start.12 = (f32[1024]{0:T(1024)S(1)}, f32[1024]{0:T(1024)}, u32[]{:S(2)}) copy-start(f32[1024]{0:T(1024)} %get-tuple-element.56) | copy-start | bytes 12292
  312.1 5.4 %copy-start.13 = (f32[1024]{0:T(1024)S(1)}, f32[1024]{0:T(1024)}, u32[]{:S(2)}) copy-start(f32[1024]{0:T(1024)} %get-tuple-element.57) | copy-start | bytes 12292
  312.1 5.4 %copy-start.14 = (f32[1024]{0:T(1024)S(1)}, f32[1024]{0:T(1024)}, u32[]{:S(2)}) copy-start(f32[1024]{0:T(1024)} %get-tuple-element.58) | copy-start | bytes 12292
  312.2 5.4 %copy-start.15 = (f32[1024]{0:T(1024)S(1)}, f32[1024]{0:T(1024)}, u32[]{:S(2)}) copy-start(f32[1024]{0:T(1024)} %get-tuple-element.59) | copy-start | bytes 12292
  457.0 5.2 %copy-start.2 = (bf16[8,1024,128]{2,1,0:T(8,128)(2,1)S(1)}, bf16[8,1024,128]{2,1,0:T(8,128)(2,1)}, u32[]{:S(2)}) copy-start(bf16[8,1024,128]{2,1,0:T(8,128)(2,1)} %param.7) | copy-start | bytes 6291460
  457.0 5.2 %copy-start.4 = (f32[8,1024,128]{2,1,0:T(8,128)S(1)}, f32[8,1024,128]{2,1,0:T(8,128)}, u32[]{:S(2)}) copy-start(f32[8,1024,128]{2,1,0:T(8,128)} %fusion.11) | copy-start | bytes 12582916
  457.0 5.2 %copy-start.5 = (f32[8,128,128]{1,2,0:T(8,128)S(1)}, f32[8,128,128]{1,2,0:T(8,128)}, u32[]{:S(2)}) copy-start(f32[8,128,128]{1,2,0:T(8,128)} %reduce-scatter.2.cloned.1.call-done) | copy-start | bytes 1572868
Sparse Core Ops, SparseCore 0:
  45.0 257.7 reduce-scatter.1
